TPU v7x, 256 devices: a whole 4x4x8 slice. The times are simulated.
256 devices in a mesh: cell: 32 (over z, y_hi, core), period: 8 (over x, y_lo).
Axes of the slice: x: 4, y: 4 (y_hi: 2, y_lo: 2; y = y_hi * 2 + y_lo), z: 8, core: 2. Of those that a mesh axis runs over, the one named last changes fastest.
Arguments:
- footprints: float32 [32, 16, 32768], P(None, 'period', 'cell'), may hold values from -16 to 16
- cell_coords: int32 [2, 32768], P(None, 'cell'), may hold values from 0 to 255, as said below
- obs_period: int32 [32], replicated, may hold values from 0 to 15
- temporal_cov: float32 [16, 16], replicated, may hold values from -1.5 to 1.5
Outputs:
- hq_field: float32 [32, 16, 32768], P(None, 'period', 'cell')
- hqh_gram: float32 [32, 32], replicated
Inputs may be any that keep to these rules, and one draw needn't show every extreme that they name: `cell_coords`: cells sit at distinct grid points that together fill the rectangle of first coordinates 0 to 255 and second coordinates 0 to 127.
All inputs are finite; a program needn't handle non-finite values.
Results may differ from a plain program's by a relative error of at most 0.0003.
Values sent between devices are 32-bit elements; how exact they have to be, the bound alone decides.
No kernel may reach another device: no remote copies, remote signals or barrier semaphores. Data moves between devices by JAX's collectives and lax.ppermute only.
A program may use at most 64 MiB of HBM per device.

v0:
```python
import jax
import jax.numpy as jnp
from jax import lax
from jax.sharding import PartitionSpec as P

LENGTH_SCALE = 48.0
BLOCK_LIMIT = 4096


def covariance_tile(first_xy, second_xy):
    delta_x = first_xy[0][:, None] - second_xy[0][None, :]
    delta_y = first_xy[1][:, None] - second_xy[1][None, :]
    return jnp.exp(-jnp.sqrt(delta_x * delta_x + delta_y * delta_y) / LENGTH_SCALE)


def block_size(total_width, unit_width):
    unit_count = total_width // unit_width
    best_count = 1
    for factor in range(1, unit_count + 1):
        if unit_count % factor == 0 and factor * unit_width <= max(BLOCK_LIMIT, unit_width):
            best_count = factor
    return best_count * unit_width


def on_device(footprints, cell_coords, obs_period, temporal_cov):
    obs_count, per_local, cell_local = footprints.shape
    flat_count = obs_count * per_local
    period_first = lax.axis_index("period") * per_local
    period_ids = period_first + jnp.arange(per_local, dtype=jnp.int32)
    keep = (period_ids[None, :, None] <= obs_period[:, None, None]).astype(jnp.float32)
    masked = footprints * keep
    flat_rows = masked.reshape(flat_count, cell_local)
    local_places = cell_coords.astype(jnp.float32)
    empty = jnp.zeros((flat_count, cell_local), jnp.float32)
    piece_rows = lax.all_gather(flat_rows, "cell", axis=1, tiled=True)
    piece_places = lax.all_gather(local_places, "cell", axis=1, tiled=True)
    piece_width = piece_rows.shape[1]
    block_width = block_size(piece_width, cell_local)

    def add_block(block_index, running_sum):
        offset = block_index * block_width
        part_rows = lax.dynamic_slice_in_dim(piece_rows, offset, block_width, 1)
        part_places = lax.dynamic_slice_in_dim(piece_places, offset, block_width, 1)
        tile = covariance_tile(part_places, local_places)
        return running_sum + jnp.dot(
            part_rows, tile, precision=lax.Precision.HIGHEST, preferred_element_type=jnp.float32
        )

    spatial_flat = lax.fori_loop(0, piece_width // block_width, add_block, empty)
    spatial = spatial_flat.reshape(obs_count, per_local, cell_local)
    piece = lax.all_gather(spatial, "period", axis=1, tiled=True)
    weights = lax.dynamic_slice(temporal_cov, (period_first, 0), (per_local, piece.shape[1]))
    hq_field = jnp.einsum("tu,nuj->ntj", weights, piece, precision=lax.Precision.HIGHEST)
    partial_gram = jnp.einsum("ntj,mtj->nm", hq_field, masked, precision=lax.Precision.HIGHEST)
    hqh_gram = lax.psum(partial_gram, ("cell", "period"))
    return (hq_field, hqh_gram)


def solution(mesh):
    return jax.shard_map(
        on_device,
        mesh=mesh,
        in_specs=(P(None, "period", "cell"), P(None, "cell"), P(), P()),
        out_specs=(P(None, "period", "cell"), P()),
        check_vma=False,
    )
```

profile of v0, /device:TPU:1, one launch (start us, length us, event | category | flops | bytes accessed | tf_op | source)
XLA Modules:
  0.0 412.7 jit_solution(13719887616135554057)
XLA Ops:
  7.2 0.7 compare_convert_fusion
  8.1 1.1 broadcast_multiply_fusion
  9.2 0.9 reshape.51
  10.1 0.7 convert_element_type.12
  10.8 47.3 %all_gather.10 = f32[2,32768]{1,0:T(2,128)S(1)} all-gather(f32[2,1024]{1,0:T(2,128)S(1)} %convert_element_type.12), channel_id=1, replica_groups=mesh['cell'=32,'period'=8] {'cell'}, dimensions={1}, use_global_device_ids=true | all-gather | bytes 270336 | tf_op jit(solution)/shard_map/all_gather | solution.py:36
  58.1 58.6 %all-gather.3.cloned.1.call-done = f32[64,32768]{1,0:T(8,128)} async-done(((f32[64,1024]{1,0:T(8,128)}), f32[64,32768]{1,0:T(8,128)}) %all-gather.3.cloned.1.call-update) | async-done | bytes 8388624 | tf_op jit(solution)/shard_map/all_gather | solution.py:35
  116.7 157.3 %while.14 = (s32[]{:T(128)}, f32[64,1024]{1,0:T(8,128)S(1)}, f32[64,32768]{1,0:T(8,128)}, f32[2,32768]{1,0:T(2,128)S(1)}, f32[2,1024]{1,0:T(2,128)S(1)}, /*index...) while((s32[]{:T(128)}, f32[64,1024]{1,0:T(8,128)S(1)}, f32[64,32768]{1,0:T(8,128)}, ...), condition=%wide.region_1.0_spmd.clone, body=%wide.region_0.0_spmd.clone.sunk | while | flops 3250716672 | bytes 1695933 | solution.py:49
  116.8 19.5 %fusion.39 = f32[64,1024]{1,0:T(8,128)S(1)} fusion(f32[1024]{0:T(1024)S(1)} %bitcast.22, f32[4096]{0:T(1024)S(1)} %bitcast.20, f32[1024]{0:T(1024)S(1)} %bitcast.21, f32[4096]{0:T(1024)S(1)} %bitcast.19, f32[64,32768]{1,0:T(8,128)} %get-tuple-element.190, s32[]{:T(128)S(6)} %select_n.14, f32[64,1024]{1,0:T(8,128)S(1)} %get-tuple-element.179, ...), kind=kOutput, calls=%fused_computation.15.clone.1 | convolution fusion | flops 3250716672 | bytes 1613829 | tf_op jit(solution)/shard_map/while/body/eval_jaxpr/dot_general | solution.py:45
  136.3 0.1 constant_dynamic-slice_fusion.2
  136.4 19.5 %fusion.39 = f32[64,1024]{1,0:T(8,128)S(1)} fusion(f32[1024]{0:T(1024)S(1)} %bitcast.22, f32[4096]{0:T(1024)S(1)} %bitcast.20, f32[1024]{0:T(1024)S(1)} %bitcast.21, f32[4096]{0:T(1024)S(1)} %bitcast.19, f32[64,32768]{1,0:T(8,128)} %get-tuple-element.190, s32[]{:T(128)S(6)} %select_n.14, f32[64,1024]{1,0:T(8,128)S(1)} %get-tuple-element.179, ...), kind=kOutput, calls=%fused_computation.15.clone.1 | convolution fusion | flops 3250716672 | bytes 1613829 | tf_op jit(solution)/shard_map/while/body/eval_jaxpr/dot_general | solution.py:45
  156.0 0.1 constant_dynamic-slice_fusion.2
  156.1 19.5 %fusion.39 = f32[64,1024]{1,0:T(8,128)S(1)} fusion(f32[1024]{0:T(1024)S(1)} %bitcast.22, f32[4096]{0:T(1024)S(1)} %bitcast.20, f32[1024]{0:T(1024)S(1)} %bitcast.21, f32[4096]{0:T(1024)S(1)} %bitcast.19, f32[64,32768]{1,0:T(8,128)} %get-tuple-element.190, s32[]{:T(128)S(6)} %select_n.14, f32[64,1024]{1,0:T(8,128)S(1)} %get-tuple-element.179, ...), kind=kOutput, calls=%fused_computation.15.clone.1 | convolution fusion | flops 3250716672 | bytes 1613829 | tf_op jit(solution)/shard_map/while/body/eval_jaxpr/dot_general | solution.py:45
  175.6 0.1 constant_dynamic-slice_fusion.2
  175.7 19.5 %fusion.39 = f32[64,1024]{1,0:T(8,128)S(1)} fusion(f32[1024]{0:T(1024)S(1)} %bitcast.22, f32[4096]{0:T(1024)S(1)} %bitcast.20, f32[1024]{0:T(1024)S(1)} %bitcast.21, f32[4096]{0:T(1024)S(1)} %bitcast.19, f32[64,32768]{1,0:T(8,128)} %get-tuple-element.190, s32[]{:T(128)S(6)} %select_n.14, f32[64,1024]{1,0:T(8,128)S(1)} %get-tuple-element.179, ...), kind=kOutput, calls=%fused_computation.15.clone.1 | convolution fusion | flops 3250716672 | bytes 1613829 | tf_op jit(solution)/shard_map/while/body/eval_jaxpr/dot_general | solution.py:45
  195.4 19.5 %fusion.39 = f32[64,1024]{1,0:T(8,128)S(1)} fusion(f32[1024]{0:T(1024)S(1)} %bitcast.22, f32[4096]{0:T(1024)S(1)} %bitcast.20, f32[1024]{0:T(1024)S(1)} %bitcast.21, f32[4096]{0:T(1024)S(1)} %bitcast.19, f32[64,32768]{1,0:T(8,128)} %get-tuple-element.190, s32[]{:T(128)S(6)} %select_n.14, f32[64,1024]{1,0:T(8,128)S(1)} %get-tuple-element.179, ...), kind=kOutput, calls=%fused_computation.15.clone.1 | convolution fusion | flops 3250716672 | bytes 1613829 | tf_op jit(solution)/shard_map/while/body/eval_jaxpr/dot_general | solution.py:45
  215.0 19.5 %fusion.39 = f32[64,1024]{1,0:T(8,128)S(1)} fusion(f32[1024]{0:T(1024)S(1)} %bitcast.22, f32[4096]{0:T(1024)S(1)} %bitcast.20, f32[1024]{0:T(1024)S(1)} %bitcast.21, f32[4096]{0:T(1024)S(1)} %bitcast.19, f32[64,32768]{1,0:T(8,128)} %get-tuple-element.190, s32[]{:T(128)S(6)} %select_n.14, f32[64,1024]{1,0:T(8,128)S(1)} %get-tuple-element.179, ...), kind=kOutput, calls=%fused_computation.15.clone.1 | convolution fusion | flops 3250716672 | bytes 1613829 | tf_op jit(solution)/shard_map/while/body/eval_jaxpr/dot_general | solution.py:45
  234.7 19.5 %fusion.39 = f32[64,1024]{1,0:T(8,128)S(1)} fusion(f32[1024]{0:T(1024)S(1)} %bitcast.22, f32[4096]{0:T(1024)S(1)} %bitcast.20, f32[1024]{0:T(1024)S(1)} %bitcast.21, f32[4096]{0:T(1024)S(1)} %bitcast.19, f32[64,32768]{1,0:T(8,128)} %get-tuple-element.190, s32[]{:T(128)S(6)} %select_n.14, f32[64,1024]{1,0:T(8,128)S(1)} %get-tuple-element.179, ...), kind=kOutput, calls=%fused_computation.15.clone.1 | convolution fusion | flops 3250716672 | bytes 1613829 | tf_op jit(solution)/shard_map/while/body/eval_jaxpr/dot_general | solution.py:45
  254.3 19.5 %fusion.39 = f32[64,1024]{1,0:T(8,128)S(1)} fusion(f32[1024]{0:T(1024)S(1)} %bitcast.22, f32[4096]{0:T(1024)S(1)} %bitcast.20, f32[1024]{0:T(1024)S(1)} %bitcast.21, f32[4096]{0:T(1024)S(1)} %bitcast.19, f32[64,32768]{1,0:T(8,128)} %get-tuple-element.190, s32[]{:T(128)S(6)} %select_n.14, f32[64,1024]{1,0:T(8,128)S(1)} %get-tuple-element.179, ...), kind=kOutput, calls=%fused_computation.15.clone.1 | convolution fusion | flops 3250716672 | bytes 1613829 | tf_op jit(solution)/shard_map/while/body/eval_jaxpr/dot_general | solution.py:45
  274.0 0.1 reshape.52
  274.2 0.8 copy.16
  275.0 48.4 %all-gather.5.cloned.1.call-done = f32[32,16,1024]{2,0,1:T(8,128)} async-done(((f32[32,2,1024]{2,0,1:T(8,128)}), f32[32,16,1024]{2,0,1:T(8,128)}) %all-gather.5.cloned.1.call-update) | async-done | bytes 2097168 | tf_op jit(solution)/shard_map/all_gather | solution.py:51
  323.4 3.9 fusion.23
  327.3 0.5 convolution_bitcast_fusion
  327.7 78.1 %psum.7 = f32[32,32]{1,0:T(8,128)} all-reduce(f32[32,32]{1,0:T(8,128)S(1)} %convolution_bitcast_fusion), channel_id=1, replica_groups=mesh['cell'=32,'period'=8] {'cell','period'}, use_global_device_ids=true, to_apply=%region_2.0 | all-reduce | flops 1024 | bytes 8192 | tf_op jit(solution)/shard_map/psum | solution.py:55
  (24 shorter events, 0.8 us)
Async XLA Ops:
  7.2 316.2 %copy-start = (f32[16,16]{1,0:T(8,128)S(1)}, f32[16,16]{1,0:T(8,128)}, u32[]{:S(2)}) copy-start(f32[16,16]{1,0:T(8,128)} %param.9) | copy-start | bytes 3076
  7.2 109.5 %all-gather.3.cloned.1.call-start = ((), (), s32[]{:S(2)}) async-start(), calls=%async_computation | async-start | bytes 8650752 | tf_op jit(solution)/shard_map/all_gather | solution.py:35
  10.1 313.3 %all-gather.5.cloned.1.call-start = ((), (), s32[]{:S(2)}) async-start(), calls=%async_computation.1 | async-start | bytes 2359296 | tf_op jit(solution)/shard_map/all_gather | solution.py:51
  327.3 78.6 %copy-start.1 = (f32[32,2,1024]{2,1,0:T(2,128)}, f32[32,2,1024]{2,1,0:T(2,128)S(1)}, u32[]{:S(2)}) copy-start(f32[32,2,1024]{2,1,0:T(2,128)S(1)} %fusion.23) | copy-start | bytes 786436
Sparse Core Ops, SparseCore 0:
  11.4 105.2 all-gather.2
  275.1 48.2 all-gather.4
where the time goes:
time: 413 us
  matrix products  160 us (39%)
  blocking collectives  125 us (30%)
  waiting for transfers between devices  107 us (26%)
  between operations  14.1 us (3%)
    dot_general x8, matrix products, add_block(): jnp.dot(part_rows, tile, precision=lax.Precision.HIGHEST, preferred_eleme...  156 us
    psum x1, blocking collectives, on_device(): hqh_gram = lax.psum(partial_gram, ('cell', 'period'))  78.1 us
    all_gather x1, waiting for transfers between devices, on_device(): piece_rows = lax.all_gather(flat_rows, 'cell', axis=1, tiled=True)  58.6 us
    all_gather x1, waiting for transfers between devices, on_device(): piece = lax.all_gather(spatial, 'period', axis=1, tiled=True)  48.4 us
    all_gather x1, blocking collectives, on_device(): piece_places = lax.all_gather(local_places, 'cell', axis=1, tiled=True)  47.3 us
  transfers between devices with their start and end apart: 2, of which 2 were waited for; matrix products, arithmetic and copies ran while one was open for 0% of the time, Pallas kernels for 0%

commit v1 on v0

--- a/solution.py
+++ b/solution.py
@@ -48,7 +48,9 @@
 
     spatial_flat = lax.fori_loop(0, piece_width // block_width, add_block, empty)
     spatial = spatial_flat.reshape(obs_count, per_local, cell_local)
-    piece = lax.all_gather(spatial, "period", axis=1, tiled=True)
+    piece = jnp.concatenate(
+        lax.all_to_all(jnp.stack([spatial] * lax.axis_size("period")), "period", 0, 0), axis=1
+    )
     weights = lax.dynamic_slice(temporal_cov, (period_first, 0), (per_local, piece.shape[1]))
     hq_field = jnp.einsum("tu,nuj->ntj", weights, piece, precision=lax.Precision.HIGHEST)
     partial_gram = jnp.einsum("ntj,mtj->nm", hq_field, masked, precision=lax.Precision.HIGHEST)

time: 413 us -> 399 us (0.966)
  waiting for transfers between devices: 107 us -> 89.8 us
  local copies, waits for them, and re-layouts: 2.84 us -> 9.42 us
    all_gather x1 -> x0, waiting for transfers between devices: 48.4 us -> none  [on_device(): piece = lax.all_gather(spatial, 'period', axis=1, tiled=True)]
    all_to_all x0 -> x1, waiting for transfers between devices: none -> 31 us  [on_device(): lax.all_to_all(jnp.stack([spatial] * lax.axis_size('period')), 'period',...]
    psum x1, blocking collectives: 78.1 us -> 73.5 us  [on_device(): hqh_gram = lax.psum(partial_gram, ('cell', 'period'))]
    reshape x2, local copies, waits for them, and re-layouts: 0.93 us -> 5.3 us  [on_device(): jnp.concatenate(lax.all_to_all(jnp.stack([spatial] * lax.axis_size('perio...]
where the time goes in v1:
time: 399 us
  matrix products  158 us (40%)
  blocking collectives  121 us (30%)
  waiting for transfers between devices  89.8 us (23%)
  between operations  14.1 us (4%)
  local copies, waits for them, and re-layouts  9.42 us (2%)
  starting transfers between devices  4.06 us (1%)
    dot_general x8, matrix products, add_block(): jnp.dot(part_rows, tile, precision=lax.Precision.HIGHEST, preferred_eleme...  156 us
    psum x1, blocking collectives, on_device(): hqh_gram = lax.psum(partial_gram, ('cell', 'period'))  73.5 us
    all_gather x1, waiting for transfers between devices, on_device(): piece_rows = lax.all_gather(flat_rows, 'cell', axis=1, tiled=True)  58.8 us
    all_gather x1, blocking collectives, on_device(): piece_places = lax.all_gather(local_places, 'cell', axis=1, tiled=True)  47.1 us
    all_to_all x1, waiting for transfers between devices, on_device(): lax.all_to_all(jnp.stack([spatial] * lax.axis_size('period')), 'period',...  31 us
  transfers between devices with their start and end apart: 2, of which 2 were waited for; matrix products, arithmetic and copies ran while one was open for 0% of the time, Pallas kernels for 0%

profile of v1, /device:TPU:1, one launch (start us, length us, event | category | flops | bytes accessed | tf_op | source)
XLA Modules:
  0.0 398.6 jit_solution(4095846216154310710)
XLA Ops:
  7.2 0.7 compare_convert_fusion
  8.1 1.1 broadcast_multiply_fusion
  9.2 0.9 reshape.56
  10.1 0.7 convert_element_type.12
  10.8 47.1 %all_gather.7 = f32[2,32768]{1,0:T(2,128)S(1)} all-gather(f32[2,1024]{1,0:T(2,128)S(1)} %convert_element_type.12), channel_id=1, replica_groups=mesh['cell'=32,'period'=8] {'cell'}, dimensions={1}, use_global_device_ids=true | all-gather | bytes 270336 | tf_op jit(solution)/shard_map/all_gather | solution.py:36
  57.9 58.8 %all-gather.2.cloned.1.call-done = f32[64,32768]{1,0:T(8,128)} async-done(((f32[64,1024]{1,0:T(8,128)}), f32[64,32768]{1,0:T(8,128)}) %all-gather.2.cloned.1.call-update) | async-done | bytes 8388624 | tf_op jit(solution)/shard_map/all_gather | solution.py:35
  116.6 157.3 %while.14 = (s32[]{:T(128)}, f32[64,1024]{1,0:T(8,128)S(1)}, f32[64,32768]{1,0:T(8,128)}, f32[2,32768]{1,0:T(2,128)S(1)}, f32[2,1024]{1,0:T(2,128)S(1)}, /*index...) while((s32[]{:T(128)}, f32[64,1024]{1,0:T(8,128)S(1)}, f32[64,32768]{1,0:T(8,128)}, ...), condition=%wide.region_1.0_spmd.clone, body=%wide.region_0.0_spmd.clone.sunk | while | flops 3250716672 | bytes 1695933 | solution.py:49
  116.8 19.5 %fusion.35 = f32[64,1024]{1,0:T(8,128)S(1)} fusion(f32[1024]{0:T(1024)S(1)} %bitcast.25, f32[4096]{0:T(1024)S(1)} %bitcast.23, f32[1024]{0:T(1024)S(1)} %bitcast.24, f32[4096]{0:T(1024)S(1)} %bitcast.22, f32[64,32768]{1,0:T(8,128)} %get-tuple-element.190, s32[]{:T(128)S(6)} %select_n.14, f32[64,1024]{1,0:T(8,128)S(1)} %get-tuple-element.179, ...), kind=kOutput, calls=%fused_computation.15.clone.1 | convolution fusion | flops 3250716672 | bytes 1613829 | tf_op jit(solution)/shard_map/while/body/eval_jaxpr/dot_general | solution.py:45
  136.4 19.5 %fusion.35 = f32[64,1024]{1,0:T(8,128)S(1)} fusion(f32[1024]{0:T(1024)S(1)} %bitcast.25, f32[4096]{0:T(1024)S(1)} %bitcast.23, f32[1024]{0:T(1024)S(1)} %bitcast.24, f32[4096]{0:T(1024)S(1)} %bitcast.22, f32[64,32768]{1,0:T(8,128)} %get-tuple-element.190, s32[]{:T(128)S(6)} %select_n.14, f32[64,1024]{1,0:T(8,128)S(1)} %get-tuple-element.179, ...), kind=kOutput, calls=%fused_computation.15.clone.1 | convolution fusion | flops 3250716672 | bytes 1613829 | tf_op jit(solution)/shard_map/while/body/eval_jaxpr/dot_general | solution.py:45
  156.1 19.5 %fusion.35 = f32[64,1024]{1,0:T(8,128)S(1)} fusion(f32[1024]{0:T(1024)S(1)} %bitcast.25, f32[4096]{0:T(1024)S(1)} %bitcast.23, f32[1024]{0:T(1024)S(1)} %bitcast.24, f32[4096]{0:T(1024)S(1)} %bitcast.22, f32[64,32768]{1,0:T(8,128)} %get-tuple-element.190, s32[]{:T(128)S(6)} %select_n.14, f32[64,1024]{1,0:T(8,128)S(1)} %get-tuple-element.179, ...), kind=kOutput, calls=%fused_computation.15.clone.1 | convolution fusion | flops 3250716672 | bytes 1613829 | tf_op jit(solution)/shard_map/while/body/eval_jaxpr/dot_general | solution.py:45
  175.7 19.5 %fusion.35 = f32[64,1024]{1,0:T(8,128)S(1)} fusion(f32[1024]{0:T(1024)S(1)} %bitcast.25, f32[4096]{0:T(1024)S(1)} %bitcast.23, f32[1024]{0:T(1024)S(1)} %bitcast.24, f32[4096]{0:T(1024)S(1)} %bitcast.22, f32[64,32768]{1,0:T(8,128)} %get-tuple-element.190, s32[]{:T(128)S(6)} %select_n.14, f32[64,1024]{1,0:T(8,128)S(1)} %get-tuple-element.179, ...), kind=kOutput, calls=%fused_computation.15.clone.1 | convolution fusion | flops 3250716672 | bytes 1613829 | tf_op jit(solution)/shard_map/while/body/eval_jaxpr/dot_general | solution.py:45
  195.4 19.5 %fusion.35 = f32[64,1024]{1,0:T(8,128)S(1)} fusion(f32[1024]{0:T(1024)S(1)} %bitcast.25, f32[4096]{0:T(1024)S(1)} %bitcast.23, f32[1024]{0:T(1024)S(1)} %bitcast.24, f32[4096]{0:T(1024)S(1)} %bitcast.22, f32[64,32768]{1,0:T(8,128)} %get-tuple-element.190, s32[]{:T(128)S(6)} %select_n.14, f32[64,1024]{1,0:T(8,128)S(1)} %get-tuple-element.179, ...), kind=kOutput, calls=%fused_computation.15.clone.1 | convolution fusion | flops 3250716672 | bytes 1613829 | tf_op jit(solution)/shard_map/while/body/eval_jaxpr/dot_general | solution.py:45
  215.0 19.5 %fusion.35 = f32[64,1024]{1,0:T(8,128)S(1)} fusion(f32[1024]{0:T(1024)S(1)} %bitcast.25, f32[4096]{0:T(1024)S(1)} %bitcast.23, f32[1024]{0:T(1024)S(1)} %bitcast.24, f32[4096]{0:T(1024)S(1)} %bitcast.22, f32[64,32768]{1,0:T(8,128)} %get-tuple-element.190, s32[]{:T(128)S(6)} %select_n.14, f32[64,1024]{1,0:T(8,128)S(1)} %get-tuple-element.179, ...), kind=kOutput, calls=%fused_computation.15.clone.1 | convolution fusion | flops 3250716672 | bytes 1613829 | tf_op jit(solution)/shard_map/while/body/eval_jaxpr/dot_general | solution.py:45
  234.6 19.5 %fusion.35 = f32[64,1024]{1,0:T(8,128)S(1)} fusion(f32[1024]{0:T(1024)S(1)} %bitcast.25, f32[4096]{0:T(1024)S(1)} %bitcast.23, f32[1024]{0:T(1024)S(1)} %bitcast.24, f32[4096]{0:T(1024)S(1)} %bitcast.22, f32[64,32768]{1,0:T(8,128)} %get-tuple-element.190, s32[]{:T(128)S(6)} %select_n.14, f32[64,1024]{1,0:T(8,128)S(1)} %get-tuple-element.179, ...), kind=kOutput, calls=%fused_computation.15.clone.1 | convolution fusion | flops 3250716672 | bytes 1613829 | tf_op jit(solution)/shard_map/while/body/eval_jaxpr/dot_general | solution.py:45
  254.3 19.5 %fusion.35 = f32[64,1024]{1,0:T(8,128)S(1)} fusion(f32[1024]{0:T(1024)S(1)} %bitcast.25, f32[4096]{0:T(1024)S(1)} %bitcast.23, f32[1024]{0:T(1024)S(1)} %bitcast.24, f32[4096]{0:T(1024)S(1)} %bitcast.22, f32[64,32768]{1,0:T(8,128)} %get-tuple-element.190, s32[]{:T(128)S(6)} %select_n.14, f32[64,1024]{1,0:T(8,128)S(1)} %get-tuple-element.179, ...), kind=kOutput, calls=%fused_computation.15.clone.1 | convolution fusion | flops 3250716672 | bytes 1613829 | tf_op jit(solution)/shard_map/while/body/eval_jaxpr/dot_general | solution.py:45
  274.0 0.1 stack_reshape.2
  274.1 2.1 stack.3
  276.2 4.0 %all-to-all-start = ((f32[8,32,2,1024]{3,2,1,0:T(2,128)}), f32[8,32,2,1024]{3,2,1,0:T(2,128)S(1)}, u32[]{:S(2)}, u32[]{:S(2)}) async-start(f32[8,32,2,1024]{3,2,1,0:T(2,128)} %stack.3), calls=%async_computation | async-start | bytes 4194304 | tf_op jit(solution)/shard_map/all_to_all | solution.py:52
  280.2 31.0 %all-to-all-done = f32[8,32,2,1024]{3,2,1,0:T(2,128)S(1)} async-done(((f32[8,32,2,1024]{3,2,1,0:T(2,128)}), f32[8,32,2,1024]{3,2,1,0:T(2,128)S(1)}, u32[]{:S(2)}, u32[]{:S(2)}) %all-to-all-start) | async-done | bytes 2097184 | tf_op jit(solution)/shard_map/all_to_all | solution.py:52
  311.2 2.6 copy.12
  313.8 2.7 reshape.58
  316.5 1.3 convolution_bitcast_fusion
  317.8 0.5 convolution_bitcast_fusion.1
  318.3 73.5 %psum.7 = f32[32,32]{1,0:T(8,128)} all-reduce(f32[32,32]{1,0:T(8,128)S(1)} %convolution_bitcast_fusion.1), channel_id=1, replica_groups=mesh['cell'=32,'period'=8] {'cell','period'}, use_global_device_ids=true, to_apply=%region_2.0 | all-reduce | flops 1024 | bytes 8192 | tf_op jit(solution)/shard_map/psum | solution.py:57
  (25 shorter events, 1.1 us)
Async XLA Ops:
  7.2 309.4 %copy-start = (f32[16,16]{1,0:T(8,128)S(1)}, f32[16,16]{1,0:T(8,128)}, u32[]{:S(2)}) copy-start(f32[16,16]{1,0:T(8,128)} %param.9) | copy-start | bytes 3076
  7.2 109.5 %all-gather.2.cloned.1.call-start = ((), (), s32[]{:S(2)}) async-start(), calls=%async_computation.1 | async-start | bytes 8650752 | tf_op jit(solution)/shard_map/all_gather | solution.py:35
  276.2 35.0 %all-to-all-start = ((f32[8,32,2,1024]{3,2,1,0:T(2,128)}), f32[8,32,2,1024]{3,2,1,0:T(2,128)S(1)}, u32[]{:S(2)}, u32[]{:S(2)}) async-start(f32[8,32,2,1024]{3,2,1,0:T(2,128)} %stack.3), calls=%async_computation | async-start | bytes 4194304 | tf_op jit(solution)/shard_map/all_to_all | solution.py:52
  317.8 74.0 %copy-start.1 = (f32[32,2,1024]{2,1,0:T(2,128)}, f32[32,2,1024]{2,1,0:T(2,128)S(1)}, u32[]{:S(2)}) copy-start(f32[32,2,1024]{2,1,0:T(2,128)S(1)} %convolution_bitcast_fusion) | copy-start | bytes 786436
Sparse Core Ops, SparseCore 0:
  11.4 105.2 all-gather.1
